TPU v7x, 512 devices: a whole 4x8x8 slice. The times are simulated.
512 devices in a mesh: leaf: 128 (over z, y, core), rhs: 4 (over x).
Axes of the slice: x: 4, y: 8, z: 8, core: 2. Of those that a mesh axis runs over, the one named last changes fastest.
Arguments:
- potential: float32 [128, 1048576], P('rhs', 'leaf'), may hold values from -6 to 6
- geometry: float32 [4, 1048576], P(None, 'leaf'), as said below
- near_count: int32 [4096], P('leaf'), may hold values from 3 to 12, as said below
- near_offset: int32 [4096, 12], P('leaf'), may hold values from -6 to 6, as said below
- far_offset: int32 [4096, 4], P('leaf'), may hold values from -8 to 8, as said below
- col_basis: bfloat16 [4096, 256, 64], P('leaf'), may hold values from -0.375 to 0.375
- row_basis: bfloat16 [4096, 256, 64], P('leaf'), may hold values from -0.5 to 0.5
- leaf_up: bfloat16 [4096, 64, 64], P('leaf'), may hold values from -0.125 to 0.125
- leaf_down: bfloat16 [4096, 64, 64], P('leaf'), may hold values from -0.75 to 0.75
- leaf_coupling: bfloat16 [4096, 4, 64, 64], P('leaf'), may hold values from -0.375 to 0.375
- up_transfer: bfloat16 [2, 64, 64], replicated, may hold values from -0.5 to 0.5
- down_transfer: bfloat16 [2, 64, 64], replicated, may hold values from -0.75 to 0.75
- sibling_coupling: bfloat16 [2, 64, 64], replicated, may hold values from -0.375 to 0.375
Outputs:
- field: float32 [128, 1048576], P('rhs', 'leaf')
Inputs may be any that keep to these rules, and one draw needn't show every extreme that they name: `geometry`: rows 0 to 2 are panel centroids, row 3 panel areas between 0.005 and 0.05. Each leaf cluster uses slots 0 to near_count - 1; some cluster uses all 12. `near_offset`: slot 0 of every cluster is the cluster itself (offset 0), slot 1 holds a positive offset and slot 2 a negative one; the other slots of a cluster hold distinct nonzero offsets. `far_offset`: every offset has magnitude above 6; the offsets of one cluster are distinct.
All inputs are finite; a program needn't handle non-finite values.
Results may differ from a plain program's by a relative error of at most 0.007.
Values may be sent and summed in bfloat16 or wider, within the bound.
No kernel may reach another device: no remote copies, remote signals or barrier semaphores. Data moves between devices by JAX's collectives and lax.ppermute only.
A program may use at most 64 MiB of HBM per device.

v0:
```python
import math
import jax
import jax.numpy as jnp
from jax import lax
from jax.sharding import PartitionSpec as P

NNEAR = 12
NWIN = 6
FWIN = 8


def with_halo(value, sides, width):
    for axis, dim in sides:
        devices, length = (lax.axis_size(axis), value.shape[dim])
        up = [(i, (i + 1) % devices) for i in range(devices - 1)]
        down = [(j, i) for i, j in up]
        last = lax.slice_in_dim(value, length - width, length, axis=dim)
        first = lax.slice_in_dim(value, 0, width, axis=dim)
        before = lax.ppermute(last, axis, up)
        after = lax.ppermute(first, axis, down)
        value = jnp.concatenate([before, value, after], axis=dim)
    return value


def from_partner(value, axis, apart):
    return lax.ppermute(value, axis, [(i, i ^ 1 << apart) for i in range(lax.axis_size(axis))])


def kernel_entries(target_geometry, source_geometry):
    squared = (target_geometry[0][:, :, None] - source_geometry[0][:, None, :]) ** 2
    squared = squared + (target_geometry[1][:, :, None] - source_geometry[1][:, None, :]) ** 2
    squared = squared + (target_geometry[2][:, :, None] - source_geometry[2][:, None, :]) ** 2
    spread = (target_geometry[3][:, :, None] + source_geometry[3][:, None, :]) / math.pi
    return source_geometry[3][:, None, :] / jnp.sqrt(squared + spread)


def select_side(table, side_bit):
    return lax.dynamic_index_in_dim(table, side_bit, 0, keepdims=False)


def per_device(
    potential,
    geometry,
    near_count,
    near_offset,
    far_offset,
    col_basis,
    row_basis,
    leaf_up,
    leaf_down,
    leaf_coupling,
    up_transfer,
    down_transfer,
    sibling_coupling,
):
    rows_here = potential.shape[0]
    clusters = near_count.shape[0]
    panels = col_basis.shape[1]
    basis_rank = col_basis.shape[2]
    partners_count = far_offset.shape[1]
    column_parts = lax.axis_size("rhs")
    per_part = clusters // column_parts
    first_local = lax.axis_index("rhs") * per_part
    window_width = per_part + 2 * NWIN
    stacked = jnp.concatenate([potential, geometry], axis=0)
    extended = with_halo(stacked, (("leaf", 1),), NWIN * panels)
    wide_rows = extended.shape[1] // panels
    value_rows = extended[:rows_here].astype(jnp.bfloat16)
    sources = lax.all_gather(value_rows, "rhs", axis=0, tiled=True)
    sources = sources.reshape(rows_here * column_parts, wide_rows, panels)
    all_rows = sources.shape[0]
    wide_geometry = extended[rows_here:].reshape(4, wide_rows, panels)
    local_geometry = lax.dynamic_slice_in_dim(wide_geometry, first_local, window_width, 1)
    target_geometry = local_geometry[:, NWIN : NWIN + per_part]
    live_counts = lax.dynamic_slice_in_dim(near_count, first_local, per_part, 0)
    offsets = lax.dynamic_slice_in_dim(near_offset, first_local, per_part, 0)
    own_clusters = NWIN + jnp.arange(per_part, dtype=jnp.int32)

    def add_slot(slot_index, running):
        shift_now = lax.dynamic_index_in_dim(offsets, slot_index, 1, keepdims=False)
        window_index = own_clusters + shift_now
        source_geometry = jnp.take(local_geometry, window_index, axis=1)
        source_values = jnp.take(sources, window_index + first_local, axis=1)
        live_mask = (slot_index < live_counts).astype(jnp.float32)
        near_block = (
            kernel_entries(target_geometry, source_geometry) * live_mask[:, None, None]
        ).astype(jnp.bfloat16)
        return running + jnp.einsum(
            "rcs,cts->rct", source_values, near_block, preferred_element_type=jnp.float32
        )

    start_sum = jnp.zeros((all_rows, per_part, panels), jnp.float32)
    near_part = lax.fori_loop(0, NNEAR, add_slot, start_sum)
    near_field = lax.all_to_all(
        near_part.reshape(all_rows, per_part * panels).astype(jnp.bfloat16),
        "rhs",
        split_axis=0,
        concat_axis=1,
        tiled=True,
    ).astype(jnp.float32)
    own_values = potential.astype(jnp.bfloat16).reshape(rows_here, clusters, panels)
    coefficients = jnp.einsum(
        "rcp,cpk->rck", own_values, col_basis, preferred_element_type=jnp.float32
    ).astype(jnp.bfloat16)
    rim_coefs = with_halo(
        coefficients.reshape(rows_here, clusters * basis_rank), (("leaf", 1),), FWIN * basis_rank
    )
    rim_coefs = rim_coefs.reshape(rows_here, clusters + 2 * FWIN, basis_rank)
    partner_index = jnp.arange(clusters, dtype=jnp.int32)[:, None] + FWIN + far_offset
    partners = jnp.take(rim_coefs, partner_index.reshape(-1), axis=1).reshape(
        rows_here, clusters, partners_count, basis_rank
    )
    leaf_far = jnp.einsum(
        "rcmk,cmkj->rcj", partners, leaf_coupling, preferred_element_type=jnp.float32
    )
    device_coef = jnp.einsum(
        "rck,ckj->rj", coefficients, leaf_up, preferred_element_type=jnp.float32
    ).astype(jnp.bfloat16)
    levels = lax.axis_size("leaf").bit_length() - 1
    device_index = lax.axis_index("leaf")
    couplings = []
    side_bits = []
    current = device_coef
    for tree_level in range(levels):
        side_bit = device_index // 2**tree_level % 2
        sibling = from_partner(current, "leaf", tree_level)
        couplings.append(
            jnp.dot(
                sibling, select_side(sibling_coupling, side_bit), preferred_element_type=jnp.float32
            )
        )
        side_bits.append(side_bit)
        if tree_level + 1 < levels:
            upward = jnp.dot(
                current, select_side(up_transfer, side_bit), preferred_element_type=jnp.float32
            )
            upward = upward + jnp.dot(
                sibling, select_side(up_transfer, 1 - side_bit), preferred_element_type=jnp.float32
            )
            current = upward.astype(jnp.bfloat16)
    local_sum = jnp.zeros((rows_here, basis_rank), jnp.float32)
    for tree_level in reversed(range(levels)):
        step_down = select_side(down_transfer, side_bits[tree_level]).astype(jnp.float32)
        local_sum = couplings[tree_level] + jnp.dot(
            local_sum, step_down, precision=lax.Precision.HIGHEST
        )
    leaf_local = leaf_far + jnp.einsum(
        "rk,ckj->rcj", local_sum, leaf_down.astype(jnp.float32), precision=lax.Precision.HIGHEST
    )
    leaf_local = leaf_local.astype(jnp.bfloat16)
    far_field = jnp.einsum(
        "rck,cpk->rcp", leaf_local, row_basis, preferred_element_type=jnp.float32
    )
    return near_field + far_field.reshape(rows_here, clusters * panels)


def solution(mesh):
    placed = (
        P("rhs", "leaf"),
        P(None, "leaf"),
        P("leaf"),
        P("leaf", None),
        P("leaf", None),
        P("leaf", None, None),
        P("leaf", None, None),
        P("leaf", None, None),
        P("leaf", None, None),
        P("leaf", None, None, None),
        P(),
        P(),
        P(),
    )
    return jax.shard_map(
        per_device, mesh=mesh, in_specs=placed, out_specs=P("rhs", "leaf"), check_vma=False
    )
```

profile of v0, /device:TPU:1, one launch (start us, length us, event | category | flops | bytes accessed | tf_op | source)
XLA Modules:
  0.0 244.2 jit_solution(15858377557532260188)
XLA Ops:
  9.3 8.8 %collective-permute-start.4 = (bf16[32,64]{1,0:T(8,128)(2,1)S(1)}, bf16[32,64]{1,0:T(8,128)(2,1)S(1)}, u32[]{:S(2)}, u32[]{:S(2)}) collective-permute-start(bf16[32,64]{1,0:T(8,128)(2,1)S(1)} %fusion.23), channel_id=1, source_target_pairs={{0,4},{4,0},{8,12},{12,8},{16,20},{20,16},{24,28},{28,24},{32,36},... | collective-permute-start | bytes 12296 | tf_op jit(solution)/shard_map/ppermute | solution.py:26
  18.9 1.9 reshape.114
  22.2 1.9 collective-permute-start.2
  24.1 3.0 %collective-permute-start.3 = (bf16[32,512]{1,0:T(8,128)(2,1)}, bf16[32,512]{1,0:T(8,128)(2,1)}, u32[]{:S(2)}, u32[]{:S(2)}) collective-permute-start(bf16[32,512]{1,0:T(8,128)(2,1)} %get-tuple-element.251), channel_id=1, source_target_pairs={{4,0},{8,4},{12,8},{16,12},{20,16},{24,20},{28,24},{32,28},{36,32}... | collective-permute-start | bytes 98312 | tf_op jit(solution)/shard_map/ppermute | solution.py:20
  28.8 2.5 %collective-permute-start = (f32[36,1536]{1,0:T(8,128)}, f32[36,1536]{1,0:T(8,128)}, u32[]{:S(2)}, u32[]{:S(2)}) collective-permute-start(f32[36,1536]{1,0:T(8,128)} %get-tuple-element.246), channel_id=1, source_target_pairs={{0,4},{4,8},{8,12},{12,16},{16,20},{20,24},{24,28},{28,32},{32,36}... | collective-permute-start | bytes 663560 | tf_op jit(solution)/shard_map/ppermute | solution.py:19
  31.4 2.4 %collective-permute-start.1 = (f32[36,1536]{1,0:T(8,128)}, f32[36,1536]{1,0:T(8,128)}, u32[]{:S(2)}, u32[]{:S(2)}) collective-permute-start(f32[36,1536]{1,0:T(8,128)} %get-tuple-element.247), channel_id=1, source_target_pairs={{4,0},{8,4},{12,8},{16,12},{20,16},{24,20},{28,24},{32,28},{36,32}... | collective-permute-start | bytes 663560 | tf_op jit(solution)/shard_map/ppermute | solution.py:20
  36.3 1.9 collective-permute-start.5
  38.3 2.7 %collective-permute-done.5 = bf16[32,64]{1,0:T(8,128)(2,1)S(1)} collective-permute-done((bf16[32,64]{1,0:T(8,128)(2,1)S(1)}, bf16[32,64]{1,0:T(8,128)(2,1)S(1)}, u32[]{:S(2)}, u32[]{:S(2)}) %collective-permute-start.5) | collective-permute-done | bytes 4128 | tf_op jit(solution)/shard_map/ppermute | solution.py:26
  41.1 1.9 collective-permute-start.6
  43.2 3.2 %collective-permute-done.6 = bf16[32,64]{1,0:T(8,128)(2,1)S(1)} collective-permute-done((bf16[32,64]{1,0:T(8,128)(2,1)S(1)}, bf16[32,64]{1,0:T(8,128)(2,1)S(1)}, u32[]{:S(2)}, u32[]{:S(2)}) %collective-permute-start.6) | collective-permute-done | bytes 4128 | tf_op jit(solution)/shard_map/ppermute | solution.py:26
  46.6 2.4 collective-permute-start.7
  49.1 5.7 %collective-permute-done.7 = bf16[32,64]{1,0:T(8,128)(2,1)S(1)} collective-permute-done((bf16[32,64]{1,0:T(8,128)(2,1)S(1)}, bf16[32,64]{1,0:T(8,128)(2,1)S(1)}, u32[]{:S(2)}, u32[]{:S(2)}) %collective-permute-start.7) | collective-permute-done | bytes 4128 | tf_op jit(solution)/shard_map/ppermute | solution.py:26
  55.6 1.9 collective-permute-start.8
  58.4 2.4 pad_maximum_fusion
  60.8 2.4 slice.115
  64.1 5.0 %collective-permute-start.9 = (bf16[32,64]{1,0:T(8,128)(2,1)S(1)}, bf16[32,64]{1,0:T(8,128)(2,1)S(1)}, u32[]{:S(2)}, u32[]{:S(2)}) collective-permute-start(bf16[32,64]{1,0:T(8,128)(2,1)S(1)} %fusion.28), channel_id=1, source_target_pairs={{0,128},{4,132},{8,136},{12,140},{16,144},{20,148},{24,152},{28,15... | collective-permute-start | bytes 12296 | tf_op jit(solution)/shard_map/ppermute | solution.py:26
  70.3 8.3 %collective-permute-start.10 = (bf16[32,64]{1,0:T(8,128)(2,1)S(1)}, bf16[32,64]{1,0:T(8,128)(2,1)S(1)}, u32[]{:S(2)}, u32[]{:S(2)}) collective-permute-start(bf16[32,64]{1,0:T(8,128)(2,1)S(1)} %fusion.29), channel_id=1, source_target_pairs={{0,256},{4,260},{8,264},{12,268},{16,272},{20,276},{24,280},{28,28... | collective-permute-start | bytes 12296 | tf_op jit(solution)/shard_map/ppermute | solution.py:26
  86.8 2.1 convolution_bitcast_fusion.2
  91.8 21.3 %all-gather.2.cloned.1.call-done = bf16[128,11264]{1,0:T(8,128)(2,1)} async-done(((bf16[32,11264]{1,0:T(8,128)(2,1)}), bf16[128,11264]{1,0:T(8,128)(2,1)}) %all-gather.2.cloned.1.call-update) | async-done | bytes 2883600 | tf_op jit(solution)/shard_map/all_gather | solution.py:69
  113.1 4.6 %copy.43 = bf16[128,11264]{0,1:T(8,128)(2,1)} copy(bf16[128,11264]{1,0:T(8,128)(2,1)} %all-gather.2.cloned.1.call-done) | data formatting | bytes 5767168 | tf_op jit(solution)/shard_map/all_gather | solution.py:69
  117.6 4.6 %copy.45 = bf16[128,44,256]{2,0,1:T(8,128)(2,1)} copy(bf16[128,44,256]{0,2,1:T(8,128)(2,1)} %bitcast.197) | data formatting | bytes 5767168
  122.2 96.9 %while.14 = (s32[]{:T(128)}, f32[128,8,256]{0,2,1:T(8,128)}, s32[8,12]{0,1:T(8,128)}, f32[4,20,256]{2,0,1:T(4,128)S(1)}, f32[4,8,256]{2,1,0:T(8,128)S(1)}, /*ind...) while((s32[]{:T(128)}, f32[128,8,256]{0,2,1:T(8,128)}, ...), condition=%wide.region_1.2_spmd.clone, body=%wide.region_0.1_spmd.clone.sunk | while | flops 142354592 | bytes 4071995 | solution.py:93
  123.6 2.4 gather_fusion.1
  126.1 2.9 %fusion.174 = f32[128,8,256]{0,2,1:T(8,128)} fusion(f32[128,8,256]{0,2,1:T(8,128)} %get-tuple-element.342, f32[8]{0:T(128)S(1)} %compare_convert_fusion.2, f32[8,256]{1,0:T(8,128)S(1)} %get-tuple-element.316, f32[8,256]{1,0:T(8,128)S(1)} %get-tuple-element.320, f32[8,256]{1,0:T(8,128)S(1)} %get-tuple-element.321, ...), kind=kOutput, calls=%fused_computation.6.clone.1 | convolution fusion | flops 142344192 | bytes 2687017 | tf_op jit(solution)/shard_map/while/body/eval_jaxpr/rcs,cts->rct/dot_general | solution.py:88
  130.5 2.4 gather_fusion.1
  132.9 4.3 %fusion.174 = f32[128,8,256]{0,2,1:T(8,128)} fusion(f32[128,8,256]{0,2,1:T(8,128)} %get-tuple-element.342, f32[8]{0:T(128)S(1)} %compare_convert_fusion.2, f32[8,256]{1,0:T(8,128)S(1)} %get-tuple-element.316, f32[8,256]{1,0:T(8,128)S(1)} %get-tuple-element.320, f32[8,256]{1,0:T(8,128)S(1)} %get-tuple-element.321, ...), kind=kOutput, calls=%fused_computation.6.clone.1 | convolution fusion | flops 142344192 | bytes 2687017 | tf_op jit(solution)/shard_map/while/body/eval_jaxpr/rcs,cts->rct/dot_general | solution.py:88
  138.6 2.4 gather_fusion.1
  141.1 4.3 %fusion.174 = f32[128,8,256]{0,2,1:T(8,128)} fusion(f32[128,8,256]{0,2,1:T(8,128)} %get-tuple-element.342, f32[8]{0:T(128)S(1)} %compare_convert_fusion.2, f32[8,256]{1,0:T(8,128)S(1)} %get-tuple-element.316, f32[8,256]{1,0:T(8,128)S(1)} %get-tuple-element.320, f32[8,256]{1,0:T(8,128)S(1)} %get-tuple-element.321, ...), kind=kOutput, calls=%fused_computation.6.clone.1 | convolution fusion | flops 142344192 | bytes 2687017 | tf_op jit(solution)/shard_map/while/body/eval_jaxpr/rcs,cts->rct/dot_general | solution.py:88
  146.8 2.4 gather_fusion.1
  149.3 4.3 %fusion.174 = f32[128,8,256]{0,2,1:T(8,128)} fusion(f32[128,8,256]{0,2,1:T(8,128)} %get-tuple-element.342, f32[8]{0:T(128)S(1)} %compare_convert_fusion.2, f32[8,256]{1,0:T(8,128)S(1)} %get-tuple-element.316, f32[8,256]{1,0:T(8,128)S(1)} %get-tuple-element.320, f32[8,256]{1,0:T(8,128)S(1)} %get-tuple-element.321, ...), kind=kOutput, calls=%fused_computation.6.clone.1 | convolution fusion | flops 142344192 | bytes 2687017 | tf_op jit(solution)/shard_map/while/body/eval_jaxpr/rcs,cts->rct/dot_general | solution.py:88
  155.0 2.4 gather_fusion.1
  157.4 4.3 %fusion.174 = f32[128,8,256]{0,2,1:T(8,128)} fusion(f32[128,8,256]{0,2,1:T(8,128)} %get-tuple-element.342, f32[8]{0:T(128)S(1)} %compare_convert_fusion.2, f32[8,256]{1,0:T(8,128)S(1)} %get-tuple-element.316, f32[8,256]{1,0:T(8,128)S(1)} %get-tuple-element.320, f32[8,256]{1,0:T(8,128)S(1)} %get-tuple-element.321, ...), kind=kOutput, calls=%fused_computation.6.clone.1 | convolution fusion | flops 142344192 | bytes 2687017 | tf_op jit(solution)/shard_map/while/body/eval_jaxpr/rcs,cts->rct/dot_general | solution.py:88
  163.2 2.4 gather_fusion.1
  165.6 4.3 %fusion.174 = f32[128,8,256]{0,2,1:T(8,128)} fusion(f32[128,8,256]{0,2,1:T(8,128)} %get-tuple-element.342, f32[8]{0:T(128)S(1)} %compare_convert_fusion.2, f32[8,256]{1,0:T(8,128)S(1)} %get-tuple-element.316, f32[8,256]{1,0:T(8,128)S(1)} %get-tuple-element.320, f32[8,256]{1,0:T(8,128)S(1)} %get-tuple-element.321, ...), kind=kOutput, calls=%fused_computation.6.clone.1 | convolution fusion | flops 142344192 | bytes 2687017 | tf_op jit(solution)/shard_map/while/body/eval_jaxpr/rcs,cts->rct/dot_general | solution.py:88
  171.4 2.4 gather_fusion.1
  173.8 4.3 %fusion.174 = f32[128,8,256]{0,2,1:T(8,128)} fusion(f32[128,8,256]{0,2,1:T(8,128)} %get-tuple-element.342, f32[8]{0:T(128)S(1)} %compare_convert_fusion.2, f32[8,256]{1,0:T(8,128)S(1)} %get-tuple-element.316, f32[8,256]{1,0:T(8,128)S(1)} %get-tuple-element.320, f32[8,256]{1,0:T(8,128)S(1)} %get-tuple-element.321, ...), kind=kOutput, calls=%fused_computation.6.clone.1 | convolution fusion | flops 142344192 | bytes 2687017 | tf_op jit(solution)/shard_map/while/body/eval_jaxpr/rcs,cts->rct/dot_general | solution.py:88
  179.6 2.4 gather_fusion.1
  182.0 4.3 %fusion.174 = f32[128,8,256]{0,2,1:T(8,128)} fusion(f32[128,8,256]{0,2,1:T(8,128)} %get-tuple-element.342, f32[8]{0:T(128)S(1)} %compare_convert_fusion.2, f32[8,256]{1,0:T(8,128)S(1)} %get-tuple-element.316, f32[8,256]{1,0:T(8,128)S(1)} %get-tuple-element.320, f32[8,256]{1,0:T(8,128)S(1)} %get-tuple-element.321, ...), kind=kOutput, calls=%fused_computation.6.clone.1 | convolution fusion | flops 142344192 | bytes 2687017 | tf_op jit(solution)/shard_map/while/body/eval_jaxpr/rcs,cts->rct/dot_general | solution.py:88
  187.8 2.4 gather_fusion.1
  190.2 4.3 %fusion.174 = f32[128,8,256]{0,2,1:T(8,128)} fusion(f32[128,8,256]{0,2,1:T(8,128)} %get-tuple-element.342, f32[8]{0:T(128)S(1)} %compare_convert_fusion.2, f32[8,256]{1,0:T(8,128)S(1)} %get-tuple-element.316, f32[8,256]{1,0:T(8,128)S(1)} %get-tuple-element.320, f32[8,256]{1,0:T(8,128)S(1)} %get-tuple-element.321, ...), kind=kOutput, calls=%fused_computation.6.clone.1 | convolution fusion | flops 142344192 | bytes 2687017 | tf_op jit(solution)/shard_map/while/body/eval_jaxpr/rcs,cts->rct/dot_general | solution.py:88
  196.0 2.4 gather_fusion.1
  198.4 4.3 %fusion.174 = f32[128,8,256]{0,2,1:T(8,128)} fusion(f32[128,8,256]{0,2,1:T(8,128)} %get-tuple-element.342, f32[8]{0:T(128)S(1)} %compare_convert_fusion.2, f32[8,256]{1,0:T(8,128)S(1)} %get-tuple-element.316, f32[8,256]{1,0:T(8,128)S(1)} %get-tuple-element.320, f32[8,256]{1,0:T(8,128)S(1)} %get-tuple-element.321, ...), kind=kOutput, calls=%fused_computation.6.clone.1 | convolution fusion | flops 142344192 | bytes 2687017 | tf_op jit(solution)/shard_map/while/body/eval_jaxpr/rcs,cts->rct/dot_general | solution.py:88
  204.2 2.4 gather_fusion.1
  206.6 4.3 %fusion.174 = f32[128,8,256]{0,2,1:T(8,128)} fusion(f32[128,8,256]{0,2,1:T(8,128)} %get-tuple-element.342, f32[8]{0:T(128)S(1)} %compare_convert_fusion.2, f32[8,256]{1,0:T(8,128)S(1)} %get-tuple-element.316, f32[8,256]{1,0:T(8,128)S(1)} %get-tuple-element.320, f32[8,256]{1,0:T(8,128)S(1)} %get-tuple-element.321, ...), kind=kOutput, calls=%fused_computation.6.clone.1 | convolution fusion | flops 142344192 | bytes 2687017 | tf_op jit(solution)/shard_map/while/body/eval_jaxpr/rcs,cts->rct/dot_general | solution.py:88
  212.4 2.4 gather_fusion.1
  214.8 4.3 %fusion.174 = f32[128,8,256]{0,2,1:T(8,128)} fusion(f32[128,8,256]{0,2,1:T(8,128)} %get-tuple-element.342, f32[8]{0:T(128)S(1)} %compare_convert_fusion.2, f32[8,256]{1,0:T(8,128)S(1)} %get-tuple-element.316, f32[8,256]{1,0:T(8,128)S(1)} %get-tuple-element.320, f32[8,256]{1,0:T(8,128)S(1)} %get-tuple-element.321, ...), kind=kOutput, calls=%fused_computation.6.clone.1 | convolution fusion | flops 142344192 | bytes 2687017 | tf_op jit(solution)/shard_map/while/body/eval_jaxpr/rcs,cts->rct/dot_general | solution.py:88
  221.9 4.1 %all-to-all-start = ((bf16[4,32,2048]{2,1,0:T(8,128)(2,1)}), bf16[4,32,2048]{2,1,0:T(8,128)(2,1)}, u32[]{:S(2)}, u32[]{:S(2)}) async-start(bf16[4,32,2048]{2,1,0:T(8,128)(2,1)} %convert_element_type.77), calls=%async_computation | async-start | bytes 1048576 | tf_op jit(solution)/shard_map/all_to_all | solution.py:94
  229.1 6.0 %all-to-all-done = bf16[4,32,2048]{2,1,0:T(8,128)(2,1)} async-done(((bf16[4,32,2048]{2,1,0:T(8,128)(2,1)}), bf16[4,32,2048]{2,1,0:T(8,128)(2,1)}, u32[]{:S(2)}, u32[]{:S(2)}) %all-to-all-start) | async-done | bytes 524320 | tf_op jit(solution)/shard_map/all_to_all | solution.py:94
  (245 shorter events, 49.1 us)
Async XLA Ops:
  6.5 80.3 %copy-start = (bf16[32,4,64,64]{3,2,1,0:T(8,128)(2,1)S(1)}, bf16[32,4,64,64]{3,2,1,0:T(8,128)(2,1)}, u32[]{:S(2)}) copy-start(bf16[32,4,64,64]{3,2,1,0:T(8,128)(2,1)} %param.24) | copy-start | bytes 3145732
  6.5 106.5 %all-gather.2.cloned.1.call-start = ((), (), s32[]{:S(2)}) async-start(), calls=%async_computation.1 | async-start | bytes 3604480 | tf_op jit(solution)/shard_map/all_gather | solution.py:69
  6.5 2.0 copy-start.3
  6.5 2.4 copy-start.5
  9.0 25.0 %copy-start.13 = (s32[32,4]{0,1:T(4,128)S(1)}, s32[32,4]{0,1:T(4,128)}, u32[]{:S(2)}) copy-start(s32[32,4]{0,1:T(4,128)} %param.19) | copy-start | bytes 1540
  9.0 26.3 %copy-start.2 = (bf16[2,64,64]{2,1,0:T(8,128)(2,1)S(1)}, bf16[2,64,64]{2,1,0:T(8,128)(2,1)}, u32[]{:S(2)}) copy-start(bf16[2,64,64]{2,1,0:T(8,128)(2,1)} %param.25) | copy-start | bytes 49156
  9.0 26.4 %copy-start.6 = (bf16[2,64,64]{2,1,0:T(8,128)(2,1)S(1)}, bf16[2,64,64]{2,1,0:T(8,128)(2,1)}, u32[]{:S(2)}) copy-start(bf16[2,64,64]{2,1,0:T(8,128)(2,1)} %param.26) | copy-start | bytes 49156
  9.0 26.5 %copy-start.12 = (s32[32,12]{0,1:T(8,128)S(1)}, s32[32,12]{0,1:T(8,128)}, u32[]{:S(2)}) copy-start(s32[32,12]{0,1:T(8,128)} %param.18) | copy-start | bytes 4612
  9.3 26.9 %collective-permute-start.4 = (bf16[32,64]{1,0:T(8,128)(2,1)S(1)}, bf16[32,64]{1,0:T(8,128)(2,1)S(1)}, u32[]{:S(2)}, u32[]{:S(2)}) collective-permute-start(bf16[32,64]{1,0:T(8,128)(2,1)S(1)} %fusion.23), channel_id=1, source_target_pairs={{0,4},{4,0},{8,12},{12,8},{16,20},{20,16},{24,28},{28,24},{32,36},... | collective-permute-start | bytes 12296 | tf_op jit(solution)/shard_map/ppermute | solution.py:26
  22.2 62.5 %collective-permute-start.2 = (bf16[32,512]{1,0:T(8,128)(2,1)}, bf16[32,512]{1,0:T(8,128)(2,1)}, u32[]{:S(2)}, u32[]{:S(2)}) collective-permute-start(bf16[32,512]{1,0:T(8,128)(2,1)} %get-tuple-element.250), channel_id=1, source_target_pairs={{0,4},{4,8},{8,12},{12,16},{16,20},{20,24},{24,28},{28,32},{32,36}... | collective-permute-start | bytes 98312 | tf_op jit(solution)/shard_map/ppermute | solution.py:19
  24.1 60.6 %collective-permute-start.3 = (bf16[32,512]{1,0:T(8,128)(2,1)}, bf16[32,512]{1,0:T(8,128)(2,1)}, u32[]{:S(2)}, u32[]{:S(2)}) collective-permute-start(bf16[32,512]{1,0:T(8,128)(2,1)} %get-tuple-element.251), channel_id=1, source_target_pairs={{4,0},{8,4},{12,8},{16,12},{20,16},{24,20},{28,24},{32,28},{36,32}... | collective-permute-start | bytes 98312 | tf_op jit(solution)/shard_map/ppermute | solution.py:20
  28.8 29.5 %collective-permute-start = (f32[36,1536]{1,0:T(8,128)}, f32[36,1536]{1,0:T(8,128)}, u32[]{:S(2)}, u32[]{:S(2)}) collective-permute-start(f32[36,1536]{1,0:T(8,128)} %get-tuple-element.246), channel_id=1, source_target_pairs={{0,4},{4,8},{8,12},{12,16},{16,20},{20,24},{24,28},{28,32},{32,36}... | collective-permute-start | bytes 663560 | tf_op jit(solution)/shard_map/ppermute | solution.py:19
  31.4 27.0 %collective-permute-start.1 = (f32[36,1536]{1,0:T(8,128)}, f32[36,1536]{1,0:T(8,128)}, u32[]{:S(2)}, u32[]{:S(2)}) collective-permute-start(f32[36,1536]{1,0:T(8,128)} %get-tuple-element.247), channel_id=1, source_target_pairs={{4,0},{8,4},{12,8},{16,12},{20,16},{24,20},{28,24},{32,28},{36,32}... | collective-permute-start | bytes 663560 | tf_op jit(solution)/shard_map/ppermute | solution.py:20
  36.2 21.3 %copy-start.8 = (bf16[32,64]{1,0:T(8,128)(2,1)}, bf16[32,64]{1,0:T(8,128)(2,1)S(1)}, u32[]{:S(2)}) copy-start(bf16[32,64]{1,0:T(8,128)(2,1)S(1)} %collective-permute-done.4) | copy-start | bytes 12292
  36.3 4.7 %collective-permute-start.5 = (bf16[32,64]{1,0:T(8,128)(2,1)S(1)}, bf16[32,64]{1,0:T(8,128)(2,1)S(1)}, u32[]{:S(2)}, u32[]{:S(2)}) collective-permute-start(bf16[32,64]{1,0:T(8,128)(2,1)S(1)} %fusion.24), channel_id=1, source_target_pairs={{0,8},{4,12},{8,0},{12,4},{16,24},{20,28},{24,16},{28,20},{32,40},... | collective-permute-start | bytes 12296 | tf_op jit(solution)/shard_map/ppermute | solution.py:26
  41.1 5.3 %collective-permute-start.6 = (bf16[32,64]{1,0:T(8,128)(2,1)S(1)}, bf16[32,64]{1,0:T(8,128)(2,1)S(1)}, u32[]{:S(2)}, u32[]{:S(2)}) collective-permute-start(bf16[32,64]{1,0:T(8,128)(2,1)S(1)} %fusion.25), channel_id=1, source_target_pairs={{0,16},{4,20},{8,24},{12,28},{16,0},{20,4},{24,8},{28,12},{32,48},... | collective-permute-start | bytes 12296 | tf_op jit(solution)/shard_map/ppermute | solution.py:26
  46.6 8.3 %collective-permute-start.7 = (bf16[32,64]{1,0:T(8,128)(2,1)S(1)}, bf16[32,64]{1,0:T(8,128)(2,1)S(1)}, u32[]{:S(2)}, u32[]{:S(2)}) collective-permute-start(bf16[32,64]{1,0:T(8,128)(2,1)S(1)} %fusion.26), channel_id=1, source_target_pairs={{0,32},{4,36},{8,40},{12,44},{16,48},{20,52},{24,56},{28,60},{32,0... | collective-permute-start | bytes 12296 | tf_op jit(solution)/shard_map/ppermute | solution.py:26
  54.9 2.7 %copy-start.10 = (bf16[32,64]{1,0:T(8,128)(2,1)}, bf16[32,64]{1,0:T(8,128)(2,1)S(1)}, u32[]{:S(2)}) copy-start(bf16[32,64]{1,0:T(8,128)(2,1)S(1)} %collective-permute-done.7) | copy-start | bytes 12292
  55.6 7.6 %collective-permute-start.8 = (bf16[32,64]{1,0:T(8,128)(2,1)}, bf16[32,64]{1,0:T(8,128)(2,1)}, u32[]{:S(2)}, u32[]{:S(2)}) collective-permute-start(bf16[32,64]{1,0:T(8,128)(2,1)} %fusion.27), channel_id=1, source_target_pairs={{0,64},{4,68},{8,72},{12,76},{16,80},{20,84},{24,88},{28,92},{32,9... | collective-permute-start | bytes 12296 | tf_op jit(solution)/shard_map/ppermute | solution.py:26
  58.4 23.8 %copy-start.7 = (bf16[2,64,64]{2,1,0:T(8,128)(2,1)S(1)}, bf16[2,64,64]{2,1,0:T(8,128)(2,1)}, u32[]{:S(2)}) copy-start(bf16[2,64,64]{2,1,0:T(8,128)(2,1)} %param.27) | copy-start | bytes 49156
  60.8 22.9 %copy-start.11 = (bf16[32,64]{1,0:T(8,128)(2,1)S(1)}, bf16[32,64]{1,0:T(8,128)(2,1)}, u32[]{:S(2)}) copy-start(bf16[32,64]{1,0:T(8,128)(2,1)} %copy-done.10) | copy-start | bytes 12292
  60.8 23.7 %copy-start.9 = (bf16[32,64]{1,0:T(8,128)(2,1)S(1)}, bf16[32,64]{1,0:T(8,128)(2,1)}, u32[]{:S(2)}) copy-start(bf16[32,64]{1,0:T(8,128)(2,1)} %copy-done.8) | copy-start | bytes 12292
  60.8 23.9 %copy-start.4 = (bf16[32,2048]{1,0:T(8,128)(2,1)S(1)}, bf16[32,2048]{1,0:T(8,128)(2,1)}, u32[]{:S(2)}) copy-start(bf16[32,2048]{1,0:T(8,128)(2,1)} %reshape.114) | copy-start | bytes 393220
  64.1 6.1 %collective-permute-start.9 = (bf16[32,64]{1,0:T(8,128)(2,1)S(1)}, bf16[32,64]{1,0:T(8,128)(2,1)S(1)}, u32[]{:S(2)}, u32[]{:S(2)}) collective-permute-start(bf16[32,64]{1,0:T(8,128)(2,1)S(1)} %fusion.28), channel_id=1, source_target_pairs={{0,128},{4,132},{8,136},{12,140},{16,144},{20,148},{24,152},{28,15... | collective-permute-start | bytes 12296 | tf_op jit(solution)/shard_map/ppermute | solution.py:26
  70.3 11.9 %collective-permute-start.10 = (bf16[32,64]{1,0:T(8,128)(2,1)S(1)}, bf16[32,64]{1,0:T(8,128)(2,1)S(1)}, u32[]{:S(2)}, u32[]{:S(2)}) collective-permute-start(bf16[32,64]{1,0:T(8,128)(2,1)S(1)} %fusion.29), channel_id=1, source_target_pairs={{0,256},{4,260},{8,264},{12,268},{16,272},{20,276},{24,280},{28,28... | collective-permute-start | bytes 12296 | tf_op jit(solution)/shard_map/ppermute | solution.py:26
  117.6 4.6 %copy-start.14 = (s32[8]{0:T(128)S(1)}, s32[8]{0:T(128)}, u32[]{:S(2)}) copy-start(s32[8]{0:T(128)} %dynamic_slice.98) | copy-start | bytes 100
  220.8 5.2 %copy-start.1 = (f32[32,32,64]{2,0,1:T(8,128)S(1)}, f32[32,32,64]{2,0,1:T(8,128)}, u32[]{:S(2)}) copy-start(f32[32,32,64]{2,0,1:T(8,128)} %convolution_bitcast_fusion.2) | copy-start | bytes 786436
  221.9 13.2 %all-to-all-start = ((bf16[4,32,2048]{2,1,0:T(8,128)(2,1)}), bf16[4,32,2048]{2,1,0:T(8,128)(2,1)}, u32[]{:S(2)}, u32[]{:S(2)}) async-start(bf16[4,32,2048]{2,1,0:T(8,128)(2,1)} %convert_element_type.77), calls=%async_computation | async-start | bytes 1048576 | tf_op jit(solution)/shard_map/all_to_all | solution.py:94
Sparse Core Ops, SparseCore 0:
  63.3 49.6 all-gather.1
where the time goes:
time: 247 us; the launch traced here: 244 us
  local copies, waits for them, and re-layouts  62.7 us (25%)
  matrix products  62.2 us (25%)
  starting transfers between devices  44.3 us (18%)
  waiting for transfers between devices  39.9 us (16%)
  other arithmetic  20.4 us (8%)
  between operations  13.9 us (6%)
    dot_general x12, matrix products, add_slot(): jnp.einsum('rcs,cts->rct', source_values, near_block, preferred_element_t...  50.4 us
    ppermute x7, starting transfers between devices, from_partner(): lax.ppermute(value, axis, [(i, i ^ 1 << apart) for i in range(lax.axis_si...  30.3 us
    gather x12, local copies, waits for them, and re-layouts, add_slot(): source_values = jnp.take(sources, window_index + first_local, axis=1)  28.7 us
    all_gather x1, waiting for transfers between devices, per_device(): sources = lax.all_gather(value_rows, 'rhs', axis=0, tiled=True)  21.3 us
    ppermute x7, waiting for transfers between devices, from_partner(): lax.ppermute(value, axis, [(i, i ^ 1 << apart) for i in range(lax.axis_si...  12.5 us
    reduce_and x12, other arithmetic, add_slot(): source_values = jnp.take(sources, window_index + first_local, axis=1)  8.28 us
    gather x12, local copies, waits for them, and re-layouts, add_slot(): source_geometry = jnp.take(local_geometry, window_index, axis=1)  6.92 us
    all_to_all x1, waiting for transfers between devices, per_device(): lax.all_to_all(near_part.reshape(all_rows, per_part * panels).astype(jnp....  6.04 us
  transfers between devices with their start and end apart: 13, of which 6 were waited for; matrix products, arithmetic and copies ran while one was open for 13% of the time, Pallas kernels for 0%

commit v1 on v0

--- a/solution.py
+++ b/solution.py
@@ -91,12 +91,20 @@
 
     start_sum = jnp.zeros((all_rows, per_part, panels), jnp.float32)
     near_part = lax.fori_loop(0, NNEAR, add_slot, start_sum)
-    near_field = lax.all_to_all(
-        near_part.reshape(all_rows, per_part * panels).astype(jnp.bfloat16),
-        "rhs",
-        split_axis=0,
-        concat_axis=1,
-        tiled=True,
+    near_field = jnp.concatenate(
+        lax.all_to_all(
+            jnp.stack(
+                jnp.split(
+                    near_part.reshape(all_rows, per_part * panels).astype(jnp.bfloat16),
+                    lax.axis_size("rhs"),
+                    axis=0,
+                )
+            ),
+            "rhs",
+            0,
+            0,
+        ),
+        axis=1,
     ).astype(jnp.float32)
     own_values = potential.astype(jnp.bfloat16).reshape(rows_here, clusters, panels)
     coefficients = jnp.einsum(

time: 247 us -> 252 us (1.020)
  local copies, waits for them, and re-layouts: 62.7 us -> 66.3 us
    another operation x0 -> x4, local copies, waits for them, and re-layouts: none -> 3.51 us  [per_device(): jnp.stack(jnp.split(near_part.reshape(all_rows, per_part * panels).astype...]
where the time goes in v1:
time: 252 us; the launch traced here: 249 us
  local copies, waits for them, and re-layouts  66.3 us (26%)
  matrix products  61.2 us (24%)
  starting transfers between devices  44.4 us (18%)
  waiting for transfers between devices  40.4 us (16%)
  other arithmetic  22.2 us (9%)
  between operations  13.9 us (6%)
    dot_general x12, matrix products, add_slot(): jnp.einsum('rcs,cts->rct', source_values, near_block, preferred_element_t...  50.4 us
    ppermute x7, starting transfers between devices, from_partner(): lax.ppermute(value, axis, [(i, i ^ 1 << apart) for i in range(lax.axis_si...  30.4 us
    gather x12, local copies, waits for them, and re-layouts, add_slot(): source_values = jnp.take(sources, window_index + first_local, axis=1)  28.7 us
    all_gather x1, waiting for transfers between devices, per_device(): sources = lax.all_gather(value_rows, 'rhs', axis=0, tiled=True)  20.9 us
    ppermute x7, waiting for transfers between devices, from_partner(): lax.ppermute(value, axis, [(i, i ^ 1 << apart) for i in range(lax.axis_si...  12.5 us
    reduce_and x12, other arithmetic, add_slot(): source_values = jnp.take(sources, window_index + first_local, axis=1)  8.26 us
    all_to_all x1, waiting for transfers between devices, per_device(): lax.all_to_all(jnp.stack(jnp.split(near_part.reshape(all_rows, per_part *...  6.94 us
    gather x12, local copies, waits for them, and re-layouts, add_slot(): source_geometry = jnp.take(local_geometry, window_index, axis=1)  6.92 us
  transfers between devices with their start and end apart: 13, of which 6 were waited for; matrix products, arithmetic and copies ran while one was open for 13% of the time, Pallas kernels for 0%

profile of v1, /device:TPU:1, one launch (start us, length us, event | category | flops | bytes accessed | tf_op | source)
XLA Modules:
  0.0 249.3 jit_solution(5405785858266732042)
XLA Ops:
  9.3 8.8 %collective-permute-start.4 = (bf16[32,64]{1,0:T(8,128)(2,1)S(1)}, bf16[32,64]{1,0:T(8,128)(2,1)S(1)}, u32[]{:S(2)}, u32[]{:S(2)}) collective-permute-start(bf16[32,64]{1,0:T(8,128)(2,1)S(1)} %fusion.23), channel_id=1, source_target_pairs={{0,4},{4,0},{8,12},{12,8},{16,20},{20,16},{24,28},{28,24},{32,36},... | collective-permute-start | bytes 12296 | tf_op jit(solution)/shard_map/ppermute | solution.py:26
  18.9 1.9 reshape.120
  22.1 1.9 collective-permute-start.2
  24.1 3.0 %collective-permute-start.3 = (bf16[32,512]{1,0:T(8,128)(2,1)}, bf16[32,512]{1,0:T(8,128)(2,1)}, u32[]{:S(2)}, u32[]{:S(2)}) collective-permute-start(bf16[32,512]{1,0:T(8,128)(2,1)} %get-tuple-element.255), channel_id=1, source_target_pairs={{4,0},{8,4},{12,8},{16,12},{20,16},{24,20},{28,24},{32,28},{36,32}... | collective-permute-start | bytes 98312 | tf_op jit(solution)/shard_map/ppermute | solution.py:20
  28.8 2.6 %collective-permute-start = (f32[36,1536]{1,0:T(8,128)}, f32[36,1536]{1,0:T(8,128)}, u32[]{:S(2)}, u32[]{:S(2)}) collective-permute-start(f32[36,1536]{1,0:T(8,128)} %get-tuple-element.246), channel_id=1, source_target_pairs={{0,4},{4,8},{8,12},{12,16},{16,20},{20,24},{24,28},{28,32},{32,36}... | collective-permute-start | bytes 663560 | tf_op jit(solution)/shard_map/ppermute | solution.py:19
  31.4 2.4 collective-permute-start.1
  36.3 1.9 collective-permute-start.5
  38.4 2.6 %collective-permute-done.5 = bf16[32,64]{1,0:T(8,128)(2,1)S(1)} collective-permute-done((bf16[32,64]{1,0:T(8,128)(2,1)S(1)}, bf16[32,64]{1,0:T(8,128)(2,1)S(1)}, u32[]{:S(2)}, u32[]{:S(2)}) %collective-permute-start.5) | collective-permute-done | bytes 4128 | tf_op jit(solution)/shard_map/ppermute | solution.py:26
  41.1 1.9 collective-permute-start.6
  43.2 3.2 %collective-permute-done.6 = bf16[32,64]{1,0:T(8,128)(2,1)S(1)} collective-permute-done((bf16[32,64]{1,0:T(8,128)(2,1)S(1)}, bf16[32,64]{1,0:T(8,128)(2,1)S(1)}, u32[]{:S(2)}, u32[]{:S(2)}) %collective-permute-start.6) | collective-permute-done | bytes 4128 | tf_op jit(solution)/shard_map/ppermute | solution.py:26
  46.5 2.5 collective-permute-start.7
  49.1 5.7 %collective-permute-done.7 = bf16[32,64]{1,0:T(8,128)(2,1)S(1)} collective-permute-done((bf16[32,64]{1,0:T(8,128)(2,1)S(1)}, bf16[32,64]{1,0:T(8,128)(2,1)S(1)}, u32[]{:S(2)}, u32[]{:S(2)}) %collective-permute-start.7) | collective-permute-done | bytes 4128 | tf_op jit(solution)/shard_map/ppermute | solution.py:26
  55.6 1.9 collective-permute-start.8
  58.4 2.4 pad_maximum_fusion
  60.8 2.4 slice.119
  64.0 5.1 %collective-permute-start.9 = (bf16[32,64]{1,0:T(8,128)(2,1)S(1)}, bf16[32,64]{1,0:T(8,128)(2,1)S(1)}, u32[]{:S(2)}, u32[]{:S(2)}) collective-permute-start(bf16[32,64]{1,0:T(8,128)(2,1)S(1)} %fusion.28), channel_id=1, source_target_pairs={{0,128},{4,132},{8,136},{12,140},{16,144},{20,148},{24,152},{28,15... | collective-permute-start | bytes 12296 | tf_op jit(solution)/shard_map/ppermute | solution.py:26
  70.3 8.3 %collective-permute-start.10 = (bf16[32,64]{1,0:T(8,128)(2,1)S(1)}, bf16[32,64]{1,0:T(8,128)(2,1)S(1)}, u32[]{:S(2)}, u32[]{:S(2)}) collective-permute-start(bf16[32,64]{1,0:T(8,128)(2,1)S(1)} %fusion.29), channel_id=1, source_target_pairs={{0,256},{4,260},{8,264},{12,268},{16,272},{20,276},{24,280},{28,28... | collective-permute-start | bytes 12296 | tf_op jit(solution)/shard_map/ppermute | solution.py:26
  87.0 2.2 convolution_bitcast_fusion.2
  92.0 20.9 %all-gather.2.cloned.1.call-done = bf16[128,11264]{1,0:T(8,128)(2,1)} async-done(((bf16[32,11264]{1,0:T(8,128)(2,1)}), bf16[128,11264]{1,0:T(8,128)(2,1)}) %all-gather.2.cloned.1.call-update) | async-done | bytes 2883600 | tf_op jit(solution)/shard_map/all_gather | solution.py:69
  112.9 4.5 %copy.51 = bf16[128,11264]{0,1:T(8,128)(2,1)} copy(bf16[128,11264]{1,0:T(8,128)(2,1)} %all-gather.2.cloned.1.call-done) | data formatting | bytes 5767168 | tf_op jit(solution)/shard_map/all_gather | solution.py:69
  117.4 4.6 %copy.53 = bf16[128,44,256]{2,0,1:T(8,128)(2,1)} copy(bf16[128,44,256]{0,2,1:T(8,128)(2,1)} %bitcast.201) | data formatting | bytes 5767168
  122.0 96.9 %while.14 = (s32[]{:T(128)}, f32[128,8,256]{0,2,1:T(8,128)}, s32[8,12]{0,1:T(8,128)}, f32[4,20,256]{2,0,1:T(4,128)S(1)}, f32[4,8,256]{2,1,0:T(8,128)S(1)}, /*ind...) while((s32[]{:T(128)}, f32[128,8,256]{0,2,1:T(8,128)}, ...), condition=%wide.region_1.2_spmd.clone, body=%wide.region_0.1_spmd.clone.sunk | while | flops 142354592 | bytes 4071995 | solution.py:93
  123.4 2.4 gather_fusion.1
  125.9 2.9 %fusion.175 = f32[128,8,256]{0,2,1:T(8,128)} fusion(f32[128,8,256]{0,2,1:T(8,128)} %get-tuple-element.346, f32[8]{0:T(128)S(1)} %compare_convert_fusion.2, f32[8,256]{1,0:T(8,128)S(1)} %get-tuple-element.320, f32[8,256]{1,0:T(8,128)S(1)} %get-tuple-element.324, f32[8,256]{1,0:T(8,128)S(1)} %get-tuple-element.325, ...), kind=kOutput, calls=%fused_computation.6.clone.1 | convolution fusion | flops 142344192 | bytes 2687017 | tf_op jit(solution)/shard_map/while/body/eval_jaxpr/rcs,cts->rct/dot_general | solution.py:88
  130.3 2.4 gather_fusion.1
  132.7 4.3 %fusion.175 = f32[128,8,256]{0,2,1:T(8,128)} fusion(f32[128,8,256]{0,2,1:T(8,128)} %get-tuple-element.346, f32[8]{0:T(128)S(1)} %compare_convert_fusion.2, f32[8,256]{1,0:T(8,128)S(1)} %get-tuple-element.320, f32[8,256]{1,0:T(8,128)S(1)} %get-tuple-element.324, f32[8,256]{1,0:T(8,128)S(1)} %get-tuple-element.325, ...), kind=kOutput, calls=%fused_computation.6.clone.1 | convolution fusion | flops 142344192 | bytes 2687017 | tf_op jit(solution)/shard_map/while/body/eval_jaxpr/rcs,cts->rct/dot_general | solution.py:88
  138.5 2.4 gather_fusion.1
  140.9 4.3 %fusion.175 = f32[128,8,256]{0,2,1:T(8,128)} fusion(f32[128,8,256]{0,2,1:T(8,128)} %get-tuple-element.346, f32[8]{0:T(128)S(1)} %compare_convert_fusion.2, f32[8,256]{1,0:T(8,128)S(1)} %get-tuple-element.320, f32[8,256]{1,0:T(8,128)S(1)} %get-tuple-element.324, f32[8,256]{1,0:T(8,128)S(1)} %get-tuple-element.325, ...), kind=kOutput, calls=%fused_computation.6.clone.1 | convolution fusion | flops 142344192 | bytes 2687017 | tf_op jit(solution)/shard_map/while/body/eval_jaxpr/rcs,cts->rct/dot_general | solution.py:88
  146.6 2.4 gather_fusion.1
  149.1 4.3 %fusion.175 = f32[128,8,256]{0,2,1:T(8,128)} fusion(f32[128,8,256]{0,2,1:T(8,128)} %get-tuple-element.346, f32[8]{0:T(128)S(1)} %compare_convert_fusion.2, f32[8,256]{1,0:T(8,128)S(1)} %get-tuple-element.320, f32[8,256]{1,0:T(8,128)S(1)} %get-tuple-element.324, f32[8,256]{1,0:T(8,128)S(1)} %get-tuple-element.325, ...), kind=kOutput, calls=%fused_computation.6.clone.1 | convolution fusion | flops 142344192 | bytes 2687017 | tf_op jit(solution)/shard_map/while/body/eval_jaxpr/rcs,cts->rct/dot_general | solution.py:88
  154.8 2.4 gather_fusion.1
  157.3 4.3 %fusion.175 = f32[128,8,256]{0,2,1:T(8,128)} fusion(f32[128,8,256]{0,2,1:T(8,128)} %get-tuple-element.346, f32[8]{0:T(128)S(1)} %compare_convert_fusion.2, f32[8,256]{1,0:T(8,128)S(1)} %get-tuple-element.320, f32[8,256]{1,0:T(8,128)S(1)} %get-tuple-element.324, f32[8,256]{1,0:T(8,128)S(1)} %get-tuple-element.325, ...), kind=kOutput, calls=%fused_computation.6.clone.1 | convolution fusion | flops 142344192 | bytes 2687017 | tf_op jit(solution)/shard_map/while/body/eval_jaxpr/rcs,cts->rct/dot_general | solution.py:88
  163.0 2.4 gather_fusion.1
  165.5 4.3 %fusion.175 = f32[128,8,256]{0,2,1:T(8,128)} fusion(f32[128,8,256]{0,2,1:T(8,128)} %get-tuple-element.346, f32[8]{0:T(128)S(1)} %compare_convert_fusion.2, f32[8,256]{1,0:T(8,128)S(1)} %get-tuple-element.320, f32[8,256]{1,0:T(8,128)S(1)} %get-tuple-element.324, f32[8,256]{1,0:T(8,128)S(1)} %get-tuple-element.325, ...), kind=kOutput, calls=%fused_computation.6.clone.1 | convolution fusion | flops 142344192 | bytes 2687017 | tf_op jit(solution)/shard_map/while/body/eval_jaxpr/rcs,cts->rct/dot_general | solution.py:88
  171.2 2.4 gather_fusion.1
  173.6 4.3 %fusion.175 = f32[128,8,256]{0,2,1:T(8,128)} fusion(f32[128,8,256]{0,2,1:T(8,128)} %get-tuple-element.346, f32[8]{0:T(128)S(1)} %compare_convert_fusion.2, f32[8,256]{1,0:T(8,128)S(1)} %get-tuple-element.320, f32[8,256]{1,0:T(8,128)S(1)} %get-tuple-element.324, f32[8,256]{1,0:T(8,128)S(1)} %get-tuple-element.325, ...), kind=kOutput, calls=%fused_computation.6.clone.1 | convolution fusion | flops 142344192 | bytes 2687017 | tf_op jit(solution)/shard_map/while/body/eval_jaxpr/rcs,cts->rct/dot_general | solution.py:88
  179.4 2.4 gather_fusion.1
  181.8 4.3 %fusion.175 = f32[128,8,256]{0,2,1:T(8,128)} fusion(f32[128,8,256]{0,2,1:T(8,128)} %get-tuple-element.346, f32[8]{0:T(128)S(1)} %compare_convert_fusion.2, f32[8,256]{1,0:T(8,128)S(1)} %get-tuple-element.320, f32[8,256]{1,0:T(8,128)S(1)} %get-tuple-element.324, f32[8,256]{1,0:T(8,128)S(1)} %get-tuple-element.325, ...), kind=kOutput, calls=%fused_computation.6.clone.1 | convolution fusion | flops 142344192 | bytes 2687017 | tf_op jit(solution)/shard_map/while/body/eval_jaxpr/rcs,cts->rct/dot_general | solution.py:88
  187.6 2.4 gather_fusion.1
  190.0 4.3 %fusion.175 = f32[128,8,256]{0,2,1:T(8,128)} fusion(f32[128,8,256]{0,2,1:T(8,128)} %get-tuple-element.346, f32[8]{0:T(128)S(1)} %compare_convert_fusion.2, f32[8,256]{1,0:T(8,128)S(1)} %get-tuple-element.320, f32[8,256]{1,0:T(8,128)S(1)} %get-tuple-element.324, f32[8,256]{1,0:T(8,128)S(1)} %get-tuple-element.325, ...), kind=kOutput, calls=%fused_computation.6.clone.1 | convolution fusion | flops 142344192 | bytes 2687017 | tf_op jit(solution)/shard_map/while/body/eval_jaxpr/rcs,cts->rct/dot_general | solution.py:88
  195.8 2.4 gather_fusion.1
  198.2 4.3 %fusion.175 = f32[128,8,256]{0,2,1:T(8,128)} fusion(f32[128,8,256]{0,2,1:T(8,128)} %get-tuple-element.346, f32[8]{0:T(128)S(1)} %compare_convert_fusion.2, f32[8,256]{1,0:T(8,128)S(1)} %get-tuple-element.320, f32[8,256]{1,0:T(8,128)S(1)} %get-tuple-element.324, f32[8,256]{1,0:T(8,128)S(1)} %get-tuple-element.325, ...), kind=kOutput, calls=%fused_computation.6.clone.1 | convolution fusion | flops 142344192 | bytes 2687017 | tf_op jit(solution)/shard_map/while/body/eval_jaxpr/rcs,cts->rct/dot_general | solution.py:88
  204.0 2.4 gather_fusion.1
  206.4 4.3 %fusion.175 = f32[128,8,256]{0,2,1:T(8,128)} fusion(f32[128,8,256]{0,2,1:T(8,128)} %get-tuple-element.346, f32[8]{0:T(128)S(1)} %compare_convert_fusion.2, f32[8,256]{1,0:T(8,128)S(1)} %get-tuple-element.320, f32[8,256]{1,0:T(8,128)S(1)} %get-tuple-element.324, f32[8,256]{1,0:T(8,128)S(1)} %get-tuple-element.325, ...), kind=kOutput, calls=%fused_computation.6.clone.1 | convolution fusion | flops 142344192 | bytes 2687017 | tf_op jit(solution)/shard_map/while/body/eval_jaxpr/rcs,cts->rct/dot_general | solution.py:88
  212.2 2.4 gather_fusion.1
  214.6 4.3 %fusion.175 = f32[128,8,256]{0,2,1:T(8,128)} fusion(f32[128,8,256]{0,2,1:T(8,128)} %get-tuple-element.346, f32[8]{0:T(128)S(1)} %compare_convert_fusion.2, f32[8,256]{1,0:T(8,128)S(1)} %get-tuple-element.320, f32[8,256]{1,0:T(8,128)S(1)} %get-tuple-element.324, f32[8,256]{1,0:T(8,128)S(1)} %get-tuple-element.325, ...), kind=kOutput, calls=%fused_computation.6.clone.1 | convolution fusion | flops 142344192 | bytes 2687017 | tf_op jit(solution)/shard_map/while/body/eval_jaxpr/rcs,cts->rct/dot_general | solution.py:88
  227.0 4.1 %all-to-all-start = ((bf16[4,32,2048]{2,1,0:T(8,128)(2,1)}), bf16[4,32,2048]{2,1,0:T(8,128)(2,1)}, u32[]{:S(2)}, u32[]{:S(2)}) async-start(bf16[4,32,2048]{2,1,0:T(8,128)(2,1)} %pad_maximum_fusion.1), calls=%async_computation | async-start | bytes 1048576 | tf_op jit(solution)/shard_map/all_to_all | solution.py:95
  233.2 6.9 %all-to-all-done = bf16[4,32,2048]{2,1,0:T(8,128)(2,1)} async-done(((bf16[4,32,2048]{2,1,0:T(8,128)(2,1)}), bf16[4,32,2048]{2,1,0:T(8,128)(2,1)}, u32[]{:S(2)}, u32[]{:S(2)}) %all-to-all-start) | async-done | bytes 524320 | tf_op jit(solution)/shard_map/all_to_all | solution.py:95
  (251 shorter events, 53.5 us)
Async XLA Ops:
  6.5 80.4 %copy-start = (bf16[32,4,64,64]{3,2,1,0:T(8,128)(2,1)S(1)}, bf16[32,4,64,64]{3,2,1,0:T(8,128)(2,1)}, u32[]{:S(2)}) copy-start(bf16[32,4,64,64]{3,2,1,0:T(8,128)(2,1)} %param.24) | copy-start | bytes 3145732
  6.5 106.4 %all-gather.2.cloned.1.call-start = ((), (), s32[]{:S(2)}) async-start(), calls=%async_computation.1 | async-start | bytes 3604480 | tf_op jit(solution)/shard_map/all_gather | solution.py:69
  6.5 2.0 copy-start.3
  6.5 2.4 copy-start.5
  9.0 25.0 %copy-start.14 = (s32[32,4]{0,1:T(4,128)S(1)}, s32[32,4]{0,1:T(4,128)}, u32[]{:S(2)}) copy-start(s32[32,4]{0,1:T(4,128)} %param.19) | copy-start | bytes 1540
  9.0 26.3 %copy-start.2 = (bf16[2,64,64]{2,1,0:T(8,128)(2,1)S(1)}, bf16[2,64,64]{2,1,0:T(8,128)(2,1)}, u32[]{:S(2)}) copy-start(bf16[2,64,64]{2,1,0:T(8,128)(2,1)} %param.25) | copy-start | bytes 49156
  9.0 26.4 %copy-start.7 = (bf16[2,64,64]{2,1,0:T(8,128)(2,1)S(1)}, bf16[2,64,64]{2,1,0:T(8,128)(2,1)}, u32[]{:S(2)}) copy-start(bf16[2,64,64]{2,1,0:T(8,128)(2,1)} %param.26) | copy-start | bytes 49156
  9.0 26.5 %copy-start.13 = (s32[32,12]{0,1:T(8,128)S(1)}, s32[32,12]{0,1:T(8,128)}, u32[]{:S(2)}) copy-start(s32[32,12]{0,1:T(8,128)} %param.18) | copy-start | bytes 4612
  9.3 26.9 %collective-permute-start.4 = (bf16[32,64]{1,0:T(8,128)(2,1)S(1)}, bf16[32,64]{1,0:T(8,128)(2,1)S(1)}, u32[]{:S(2)}, u32[]{:S(2)}) collective-permute-start(bf16[32,64]{1,0:T(8,128)(2,1)S(1)} %fusion.23), channel_id=1, source_target_pairs={{0,4},{4,0},{8,12},{12,8},{16,20},{20,16},{24,28},{28,24},{32,36},... | collective-permute-start | bytes 12296 | tf_op jit(solution)/shard_map/ppermute | solution.py:26
  22.1 62.7 %collective-permute-start.2 = (bf16[32,512]{1,0:T(8,128)(2,1)}, bf16[32,512]{1,0:T(8,128)(2,1)}, u32[]{:S(2)}, u32[]{:S(2)}) collective-permute-start(bf16[32,512]{1,0:T(8,128)(2,1)} %get-tuple-element.254), channel_id=1, source_target_pairs={{0,4},{4,8},{8,12},{12,16},{16,20},{20,24},{24,28},{28,32},{32,36}... | collective-permute-start | bytes 98312 | tf_op jit(solution)/shard_map/ppermute | solution.py:19
  24.1 60.8 %collective-permute-start.3 = (bf16[32,512]{1,0:T(8,128)(2,1)}, bf16[32,512]{1,0:T(8,128)(2,1)}, u32[]{:S(2)}, u32[]{:S(2)}) collective-permute-start(bf16[32,512]{1,0:T(8,128)(2,1)} %get-tuple-element.255), channel_id=1, source_target_pairs={{4,0},{8,4},{12,8},{16,12},{20,16},{24,20},{28,24},{32,28},{36,32}... | collective-permute-start | bytes 98312 | tf_op jit(solution)/shard_map/ppermute | solution.py:20
  28.8 29.5 %collective-permute-start = (f32[36,1536]{1,0:T(8,128)}, f32[36,1536]{1,0:T(8,128)}, u32[]{:S(2)}, u32[]{:S(2)}) collective-permute-start(f32[36,1536]{1,0:T(8,128)} %get-tuple-element.246), channel_id=1, source_target_pairs={{0,4},{4,8},{8,12},{12,16},{16,20},{20,24},{24,28},{28,32},{32,36}... | collective-permute-start | bytes 663560 | tf_op jit(solution)/shard_map/ppermute | solution.py:19
  31.4 27.0 %collective-permute-start.1 = (f32[36,1536]{1,0:T(8,128)}, f32[36,1536]{1,0:T(8,128)}, u32[]{:S(2)}, u32[]{:S(2)}) collective-permute-start(f32[36,1536]{1,0:T(8,128)} %get-tuple-element.247), channel_id=1, source_target_pairs={{4,0},{8,4},{12,8},{16,12},{20,16},{24,20},{28,24},{32,28},{36,32}... | collective-permute-start | bytes 663560 | tf_op jit(solution)/shard_map/ppermute | solution.py:20
  36.2 21.3 %copy-start.9 = (bf16[32,64]{1,0:T(8,128)(2,1)}, bf16[32,64]{1,0:T(8,128)(2,1)S(1)}, u32[]{:S(2)}) copy-start(bf16[32,64]{1,0:T(8,128)(2,1)S(1)} %collective-permute-done.4) | copy-start | bytes 12292
  36.3 4.7 %collective-permute-start.5 = (bf16[32,64]{1,0:T(8,128)(2,1)S(1)}, bf16[32,64]{1,0:T(8,128)(2,1)S(1)}, u32[]{:S(2)}, u32[]{:S(2)}) collective-permute-start(bf16[32,64]{1,0:T(8,128)(2,1)S(1)} %fusion.24), channel_id=1, source_target_pairs={{0,8},{4,12},{8,0},{12,4},{16,24},{20,28},{24,16},{28,20},{32,40},... | collective-permute-start | bytes 12296 | tf_op jit(solution)/shard_map/ppermute | solution.py:26
  41.1 5.3 %collective-permute-start.6 = (bf16[32,64]{1,0:T(8,128)(2,1)S(1)}, bf16[32,64]{1,0:T(8,128)(2,1)S(1)}, u32[]{:S(2)}, u32[]{:S(2)}) collective-permute-start(bf16[32,64]{1,0:T(8,128)(2,1)S(1)} %fusion.25), channel_id=1, source_target_pairs={{0,16},{4,20},{8,24},{12,28},{16,0},{20,4},{24,8},{28,12},{32,48},... | collective-permute-start | bytes 12296 | tf_op jit(solution)/shard_map/ppermute | solution.py:26
  46.5 8.3 %collective-permute-start.7 = (bf16[32,64]{1,0:T(8,128)(2,1)S(1)}, bf16[32,64]{1,0:T(8,128)(2,1)S(1)}, u32[]{:S(2)}, u32[]{:S(2)}) collective-permute-start(bf16[32,64]{1,0:T(8,128)(2,1)S(1)} %fusion.26), channel_id=1, source_target_pairs={{0,32},{4,36},{8,40},{12,44},{16,48},{20,52},{24,56},{28,60},{32,0... | collective-permute-start | bytes 12296 | tf_op jit(solution)/shard_map/ppermute | solution.py:26
  54.8 2.7 %copy-start.11 = (bf16[32,64]{1,0:T(8,128)(2,1)}, bf16[32,64]{1,0:T(8,128)(2,1)S(1)}, u32[]{:S(2)}) copy-start(bf16[32,64]{1,0:T(8,128)(2,1)S(1)} %collective-permute-done.7) | copy-start | bytes 12292
  55.6 7.6 %collective-permute-start.8 = (bf16[32,64]{1,0:T(8,128)(2,1)}, bf16[32,64]{1,0:T(8,128)(2,1)}, u32[]{:S(2)}, u32[]{:S(2)}) collective-permute-start(bf16[32,64]{1,0:T(8,128)(2,1)} %fusion.27), channel_id=1, source_target_pairs={{0,64},{4,68},{8,72},{12,76},{16,80},{20,84},{24,88},{28,92},{32,9... | collective-permute-start | bytes 12296 | tf_op jit(solution)/shard_map/ppermute | solution.py:26
  58.3 24.0 %copy-start.8 = (bf16[2,64,64]{2,1,0:T(8,128)(2,1)S(1)}, bf16[2,64,64]{2,1,0:T(8,128)(2,1)}, u32[]{:S(2)}) copy-start(bf16[2,64,64]{2,1,0:T(8,128)(2,1)} %param.27) | copy-start | bytes 49156
  60.8 23.1 %copy-start.12 = (bf16[32,64]{1,0:T(8,128)(2,1)S(1)}, bf16[32,64]{1,0:T(8,128)(2,1)}, u32[]{:S(2)}) copy-start(bf16[32,64]{1,0:T(8,128)(2,1)} %copy-done.11) | copy-start | bytes 12292
  60.8 23.9 %copy-start.10 = (bf16[32,64]{1,0:T(8,128)(2,1)S(1)}, bf16[32,64]{1,0:T(8,128)(2,1)}, u32[]{:S(2)}) copy-start(bf16[32,64]{1,0:T(8,128)(2,1)} %copy-done.9) | copy-start | bytes 12292
  60.8 24.1 %copy-start.4 = (bf16[32,2048]{1,0:T(8,128)(2,1)S(1)}, bf16[32,2048]{1,0:T(8,128)(2,1)}, u32[]{:S(2)}) copy-start(bf16[32,2048]{1,0:T(8,128)(2,1)} %reshape.120) | copy-start | bytes 393220
  64.0 6.1 %collective-permute-start.9 = (bf16[32,64]{1,0:T(8,128)(2,1)S(1)}, bf16[32,64]{1,0:T(8,128)(2,1)S(1)}, u32[]{:S(2)}, u32[]{:S(2)}) collective-permute-start(bf16[32,64]{1,0:T(8,128)(2,1)S(1)} %fusion.28), channel_id=1, source_target_pairs={{0,128},{4,132},{8,136},{12,140},{16,144},{20,148},{24,152},{28,15... | collective-permute-start | bytes 12296 | tf_op jit(solution)/shard_map/ppermute | solution.py:26
  70.3 12.1 %collective-permute-start.10 = (bf16[32,64]{1,0:T(8,128)(2,1)S(1)}, bf16[32,64]{1,0:T(8,128)(2,1)S(1)}, u32[]{:S(2)}, u32[]{:S(2)}) collective-permute-start(bf16[32,64]{1,0:T(8,128)(2,1)S(1)} %fusion.29), channel_id=1, source_target_pairs={{0,256},{4,260},{8,264},{12,268},{16,272},{20,276},{24,280},{28,28... | collective-permute-start | bytes 12296 | tf_op jit(solution)/shard_map/ppermute | solution.py:26
  117.4 4.6 %copy-start.15 = (s32[8]{0:T(128)S(1)}, s32[8]{0:T(128)}, u32[]{:S(2)}) copy-start(s32[8]{0:T(128)} %dynamic_slice.98) | copy-start | bytes 100
  221.8 9.3 %copy-start.1 = (f32[32,32,64]{2,0,1:T(8,128)S(1)}, f32[32,32,64]{2,0,1:T(8,128)}, u32[]{:S(2)}) copy-start(f32[32,32,64]{2,0,1:T(8,128)} %convolution_bitcast_fusion.2) | copy-start | bytes 786436
  225.2 6.0 %copy-start.6 = (bf16[32,64,64]{2,1,0:T(8,128)(2,1)S(1)}, bf16[32,64,64]{2,1,0:T(8,128)(2,1)}, u32[]{:S(2)}) copy-start(bf16[32,64,64]{2,1,0:T(8,128)(2,1)} %param.23) | copy-start | bytes 786436
  227.0 13.1 %all-to-all-start = ((bf16[4,32,2048]{2,1,0:T(8,128)(2,1)}), bf16[4,32,2048]{2,1,0:T(8,128)(2,1)}, u32[]{:S(2)}, u32[]{:S(2)}) async-start(bf16[4,32,2048]{2,1,0:T(8,128)(2,1)} %pad_maximum_fusion.1), calls=%async_computation | async-start | bytes 1048576 | tf_op jit(solution)/shard_map/all_to_all | solution.py:95
Sparse Core Ops, SparseCore 0:
  63.3 49.5 all-gather.1
